TPU v7x, 256 devices: a whole 4x4x8 slice. The times are simulated.
256 devices in a mesh: col: 8 (over z), row: 32 (over y, x, core).
Axes of the slice: x: 4, y: 4, z: 8, core: 2. Of those that a mesh axis runs over, the one named last changes fastest.
Arguments:
- queries: bfloat16 [262144, 256], P(('col', 'row')), may hold values from -6 to 6
- keys: bfloat16 [262144, 256], P(('col', 'row')), may hold values from -6 to 6
- values: bfloat16 [262144, 256], P(('col', 'row')), may hold values from -6 to 6
- out_grad: bfloat16 [262144, 256], P(('col', 'row')), may hold values from -6 to 6
- weight_table: float32 [64, 2, 21], replicated, may hold values from 0.25 to 2
- profile: int32 [262144], P(('col', 'row')), may hold values from 0 to 63
Outputs:
- output: float32 [262144, 256], P(('col', 'row'))
- query_grad: float32 [262144, 256], P(('col', 'row'))
- key_grad: float32 [262144, 256], P(('col', 'row'))
- value_grad: float32 [262144, 256], P(('col', 'row'))
All inputs are finite; a program needn't handle non-finite values.
Results may differ from a plain program's by a relative error of at most 0.0034.
Values sent between devices are 32-bit elements; how exact they have to be, the bound alone decides.
No kernel may reach another device: no remote copies, remote signals or barrier semaphores. Data moves between devices by JAX's collectives and lax.ppermute only.
A program may use at most 128 MiB of HBM per device.

v0:
```python
import math

import jax
import jax.numpy as jnp
from jax import lax
from jax.sharding import PartitionSpec as P

HIGHEST_PRECISION = lax.Precision.HIGHEST


def from_partner(x, axis, distance):
    return lax.ppermute(x, axis, [(i, i ^ 1 << distance) for i in range(lax.axis_size(axis))])


def digit_count(numbers, count):
    total = jnp.zeros_like(numbers)
    for digit_place in range(count):
        total = total + (numbers >= 1 << digit_place).astype(jnp.int32)
    return total


def level_weights(weight_table, profile, head_width):
    table_rows = weight_table.shape[0]
    onehot = (profile[:, None] == jnp.arange(table_rows, dtype=jnp.int32)[None, :]).astype(
        jnp.float32
    )
    flat_table = weight_table.reshape(table_rows, -1)
    picked = jnp.dot(
        onehot, flat_table, precision=HIGHEST_PRECISION, preferred_element_type=jnp.float32
    )
    picked = picked.reshape(profile.shape[0], weight_table.shape[1], weight_table.shape[2])
    depth = jnp.arange(weight_table.shape[2], dtype=jnp.float32)
    scaling = jnp.exp2(-0.5 * depth) / math.sqrt(head_width)
    return picked * scaling


def upper_half(own_index, bit_place):
    return (own_index >> bit_place & 1).astype(jnp.float32)


def fenwick_states(tile_state, grad_state, row_bits, col_bits):
    row_index = lax.axis_index("row")
    col_index = lax.axis_index("col")
    buckets = []
    pulled = jnp.zeros_like(tile_state)
    carried = tile_state
    stacked = grad_state
    for bit_place in range(row_bits):
        other_carried, other_stack = from_partner((carried, stacked), "row", bit_place)
        upper = upper_half(row_index, bit_place)
        buckets.append(upper * other_carried)
        pulled = pulled + (1.0 - upper) * other_stack[0]
        carried = carried + other_carried
        stacked = stacked[1:] + other_stack[1:]
    row_total = carried
    row_stack = stacked
    carried = row_total
    stacked = row_stack
    for bit_place in range(col_bits):
        other_carried, other_stack = from_partner((carried, stacked), "col", bit_place)
        upper = upper_half(col_index, bit_place)
        buckets.append(upper * other_carried)
        pulled = pulled + (1.0 - upper) * other_stack[0]
        carried = carried + other_carried
        stacked = stacked[1:] + other_stack[1:]
    return (jnp.stack(buckets, axis=0), pulled)


def local_attention(query_heads, key_heads, value_heads, grad_heads, weights, tile_bits):
    token_count = query_heads.shape[0]
    head_count = query_heads.shape[1]
    span = min(token_count, 512)
    out_parts = []
    query_parts = []
    key_total = jnp.zeros(key_heads.shape, jnp.float32)
    value_total = jnp.zeros(value_heads.shape, jnp.float32)
    for block_start in range(0, token_count, span):
        block_end = block_start + span
        row_places = jnp.arange(block_start, block_end, dtype=jnp.int32)
        col_places = jnp.arange(block_end, dtype=jnp.int32)
        levels = digit_count(jnp.bitwise_xor(row_places[:, None], col_places[None, :]), tile_bits)
        causal = col_places[None, :] <= row_places[:, None]
        block_weights = weights[block_start:block_end]
        level_mask = jnp.zeros((head_count, span, block_end), jnp.float32)
        for level in range(tile_bits + 1):
            level_mask = level_mask + jnp.where(
                levels[None] == level, jnp.transpose(block_weights[:, :, level])[:, :, None], 0.0
            )
        level_mask = jnp.where(causal[None], level_mask, 0.0)
        query_block = query_heads[block_start:block_end]
        grad_block = grad_heads[block_start:block_end]
        key_front = key_heads[:block_end]
        value_front = value_heads[:block_end]
        scores = jnp.einsum(
            "thd,shd->hts", query_block, key_front, preferred_element_type=jnp.float32
        )
        local_probs = (scores * level_mask).astype(jnp.bfloat16)
        out_parts.append(
            jnp.einsum("hts,she->the", local_probs, value_front, preferred_element_type=jnp.float32)
        )
        grad_scores = jnp.einsum(
            "the,she->hts", grad_block, value_front, preferred_element_type=jnp.float32
        )
        local_grad = (grad_scores * level_mask).astype(jnp.bfloat16)
        query_parts.append(
            jnp.einsum("hts,shd->thd", local_grad, key_front, preferred_element_type=jnp.float32)
        )
        key_total = key_total.at[:block_end].add(
            jnp.einsum("hts,thd->shd", local_grad, query_block, preferred_element_type=jnp.float32)
        )
        value_total = value_total.at[:block_end].add(
            jnp.einsum("hts,the->she", local_probs, grad_block, preferred_element_type=jnp.float32)
        )
    return (
        jnp.concatenate(out_parts, axis=0),
        jnp.concatenate(query_parts, axis=0),
        key_total,
        value_total,
    )


def shards(queries, keys, values, out_grad, weight_table, profile):
    token_count = queries.shape[0]
    head_count = weight_table.shape[1]
    head_width = queries.shape[1] // head_count
    tile_bits = token_count.bit_length() - 1
    row_bits = lax.axis_size("row").bit_length() - 1
    col_bits = lax.axis_size("col").bit_length() - 1
    far_levels = row_bits + col_bits
    weights = level_weights(weight_table, profile, head_width)
    far_weights = weights[:, :, tile_bits + 1 : tile_bits + 1 + far_levels]
    head_shape = (token_count, head_count, head_width)
    query_heads = queries.reshape(head_shape)
    key_heads = keys.reshape(head_shape)
    value_heads = values.reshape(head_shape)
    grad_heads = out_grad.reshape(head_shape)
    tile_state = jnp.einsum(
        "thd,the->hde", key_heads, value_heads, preferred_element_type=jnp.float32
    )
    weighted = (query_heads.astype(jnp.float32)[:, :, None, :] * far_weights[..., None]).astype(
        jnp.bfloat16
    )
    grad_state = jnp.einsum(
        "thld,the->lhde", weighted, grad_heads, preferred_element_type=jnp.float32
    )
    local_out, local_dq, local_dk, local_dv = local_attention(
        query_heads, key_heads, value_heads, grad_heads, weights, tile_bits
    )
    bucket, pulled = fenwick_states(tile_state, grad_state, row_bits, col_bits)
    bucket_half = bucket.astype(jnp.bfloat16)
    pulled_half = pulled.astype(jnp.bfloat16)
    reach = jnp.einsum(
        "thd,lhde->thle", query_heads, bucket_half, preferred_element_type=jnp.float32
    )
    far_out = jnp.sum(reach * far_weights[..., None], axis=2)
    back = jnp.einsum("the,lhde->thld", grad_heads, bucket_half, preferred_element_type=jnp.float32)
    far_dq = jnp.sum(back * far_weights[..., None], axis=2)
    far_dk = jnp.einsum(
        "the,hde->thd", value_heads, pulled_half, preferred_element_type=jnp.float32
    )
    far_dv = jnp.einsum("thd,hde->the", key_heads, pulled_half, preferred_element_type=jnp.float32)
    flat_shape = (token_count, head_count * head_width)
    output = (local_out + far_out).reshape(flat_shape)
    query_grad = (local_dq + far_dq).reshape(flat_shape)
    key_grad = (local_dk + far_dk).reshape(flat_shape)
    value_grad = (local_dv + far_dv).reshape(flat_shape)
    return (output, query_grad, key_grad, value_grad)


def solution(mesh):
    in_specs = (
        P(("col", "row"), None),
        P(("col", "row"), None),
        P(("col", "row"), None),
        P(("col", "row"), None),
        P(),
        P(("col", "row")),
    )
    out_specs = (
        P(("col", "row"), None),
        P(("col", "row"), None),
        P(("col", "row"), None),
        P(("col", "row"), None),
    )
    return jax.shard_map(shards, mesh=mesh, in_specs=in_specs, out_specs=out_specs, check_vma=False)
```

profile of v0, /device:TPU:2, one launch (start us, length us, event | category | flops | bytes accessed | tf_op | source)
XLA Modules:
  0.0 194.4 jit_solution(13251020580575505565)
XLA Ops:
  2.4 1.2 reshape.654
  5.2 2.2 %fusion.19 = f32[8,2,128,128]{3,2,0,1:T(8,128)} fusion(f32[1024,2,128]{0,2,1:T(8,128)S(1)} %convert_element_type.1223, f32[1024,2,8]{0,2,1:T(8,128)S(1)} %slice.350, bf16[1024,2,128,1]{2,1,0,3:T(2,128)(2,1)S(1)} %bitcast.267), kind=kOutput, calls=%fused_computation.35 | convolution fusion | flops 541065216 | bytes 2686976 | tf_op jit(solution)/shard_map/thld,the->lhde/dot_general | solution.py:143
  11.3 1.1 iota_compare_fusion.1
  12.4 1.2 broadcast_compare_fusion.12
  13.5 1.2 broadcast_compare_fusion.14
  14.7 1.2 broadcast_compare_fusion.16
  15.9 1.2 broadcast_compare_fusion.18
  17.0 1.2 broadcast_compare_fusion.20
  18.9 7.7 %iota_compare_fusion = (pred[512,1024]{1,0:T(8,128)(4,1)S(1)}, pred[512,1024]{1,0:T(8,128)(4,1)S(1)}, pred[512,1024]{1,0:T(8,128)(4,1)}, pred[512,1024]{1,0:T(8,...) fusion(s32[512]{0:T(512)S(1)} %iota_add_fusion), kind=kLoop, calls=%fused_computation.24 | loop fusion | flops 22020096 | bytes 6293504 | tf_op jit(solution)/shard_map/le | solution.py:82
  32.7 4.6 %add_select_fusion.1 = f32[2,512,512]{2,1,0:T(8,128)S(1)} fusion(f32[2,512]{1,0:T(2,128)S(1)} %get-tuple-element.129, f32[2,512]{1,0:T(2,128)S(1)} %get-tuple-element.130, f32[2,512]{1,0:T(2,128)S(1)} %get-tuple-element.131, f32[2,512]{1,0:T(2,128)S(1)} %get-tuple-element.132, f32[2,512]{1,0:T(2,128)S(1)} %get-tuple-element.133, ...), kind=kLoop, calls=%fused_computation.26 | loop fusion | flops 11534336 | bytes 5287936 | tf_op jit(solution)/shard_map/jit(_where)/select_n | solution.py:89
  40.7 7.2 %add_select_fusion = f32[2,512,1024]{2,1,0:T(8,128)S(1)} fusion(f32[2,512]{1,0:T(2,128)S(1)} %get-tuple-element.118, f32[2,512]{1,0:T(2,128)S(1)} %get-tuple-element.119, f32[2,512]{1,0:T(2,128)S(1)} %get-tuple-element.120, f32[2,512]{1,0:T(2,128)S(1)} %get-tuple-element.121, f32[2,512]{1,0:T(2,128)S(1)} %get-tuple-element.122, ...), kind=kLoop, calls=%fused_computation.10 | loop fusion | flops 23068672 | bytes 10530816 | tf_op jit(solution)/shard_map/jit(_where)/select_n | solution.py:89
  48.9 1.6 fusion.84
  51.3 1.6 slice_add_fusion
  52.9 2.3 %collective-permute-start.9 = (f32[7,2,128,128]{3,2,0,1:T(8,128)S(1)}, f32[7,2,128,128]{3,2,0,1:T(8,128)S(1)}, u32[]{:S(2)}, u32[]{:S(2)}) collective-permute-start(f32[7,2,128,128]{3,2,0,1:T(8,128)S(1)} %slice_add_fusion), channel_id=1, source_target_pairs={{0,2},{1,3},{2,0},{3,1},{4,6},{5,7},{6,4},{7,5},{8,10},{9,11},{10,... | collective-permute-start | bytes 2752520 | tf_op jit(solution)/shard_map/ppermute | solution.py:12
  55.2 1.6 fusion.30
  56.8 1.4 fusion.18
  58.3 1.4 fusion.17
  59.7 16.0 %collective-permute-done.9 = f32[7,2,128,128]{3,2,0,1:T(8,128)S(1)} collective-permute-done((f32[7,2,128,128]{3,2,0,1:T(8,128)S(1)}, f32[7,2,128,128]{3,2,0,1:T(8,128)S(1)}, u32[]{:S(2)}, u32[]{:S(2)}) %collective-permute-start.9) | collective-permute-done | bytes 917536 | tf_op jit(solution)/shard_map/ppermute | solution.py:12
  75.8 1.9 collective-permute-start.10
  78.8 2.1 %copy.97 = f32[512,256]{1,0:T(8,128)} copy(f32[512,256]{0,1:T(8,128)} %bitcast.263) | data formatting | bytes 1048576 | tf_op jit(solution)/shard_map/concatenate | solution.py:116
  84.9 1.5 collective-permute-start.1
  86.4 12.2 %collective-permute-done.1 = f32[2,128,128]{2,1,0:T(8,128)S(1)} collective-permute-done((f32[2,128,128]{2,1,0:T(8,128)S(1)}, f32[2,128,128]{2,1,0:T(8,128)S(1)}, u32[]{:S(2)}, u32[]{:S(2)}) %collective-permute-start.1) | collective-permute-done | bytes 131104 | tf_op jit(solution)/shard_map/ppermute | solution.py:12
  98.6 1.7 collective-permute-start.2
  100.3 4.8 %collective-permute-done.2 = f32[2,128,128]{2,1,0:T(8,128)S(1)} collective-permute-done((f32[2,128,128]{2,1,0:T(8,128)S(1)}, f32[2,128,128]{2,1,0:T(8,128)S(1)}, u32[]{:S(2)}, u32[]{:S(2)}) %collective-permute-start.2) | collective-permute-done | bytes 131104 | tf_op jit(solution)/shard_map/ppermute | solution.py:12
  105.2 1.7 collective-permute-start.3
  106.8 1.2 slice_add_fusion.2
  108.6 3.1 %collective-permute-done.3 = f32[2,128,128]{2,1,0:T(8,128)S(1)} collective-permute-done((f32[2,128,128]{2,1,0:T(8,128)S(1)}, f32[2,128,128]{2,1,0:T(8,128)S(1)}, u32[]{:S(2)}, u32[]{:S(2)}) %collective-permute-start.3) | collective-permute-done | bytes 131104 | tf_op jit(solution)/shard_map/ppermute | solution.py:12
  111.6 3.3 %collective-permute-start.4 = (f32[2,128,128]{2,1,0:T(8,128)S(1)}, f32[2,128,128]{2,1,0:T(8,128)S(1)}, u32[]{:S(2)}, u32[]{:S(2)}) collective-permute-start(f32[2,128,128]{2,1,0:T(8,128)S(1)} %add.1279), channel_id=1, source_target_pairs={{0,16},{1,17},{2,18},{3,19},{4,20},{5,21},{6,22},{7,23},{8,24},{9,... | collective-permute-start | bytes 393224 | tf_op jit(solution)/shard_map/ppermute | solution.py:12
  115.0 12.6 %collective-permute-done.4 = f32[2,128,128]{2,1,0:T(8,128)S(1)} collective-permute-done((f32[2,128,128]{2,1,0:T(8,128)S(1)}, f32[2,128,128]{2,1,0:T(8,128)S(1)}, u32[]{:S(2)}, u32[]{:S(2)}) %collective-permute-start.4) | collective-permute-done | bytes 131104 | tf_op jit(solution)/shard_map/ppermute | solution.py:12
  127.5 2.0 %collective-permute-start.5 = (f32[2,128,128]{2,1,0:T(8,128)S(1)}, f32[2,128,128]{2,1,0:T(8,128)S(1)}, u32[]{:S(2)}, u32[]{:S(2)}) collective-permute-start(f32[2,128,128]{2,1,0:T(8,128)S(1)} %add.1280), channel_id=1, source_target_pairs={{0,32},{32,0},{64,96},{96,64},{128,160},{160,128},{192,224},{224,1... | collective-permute-start | bytes 393224 | tf_op jit(solution)/shard_map/ppermute | solution.py:12
  129.6 4.2 %collective-permute-done.5 = f32[2,128,128]{2,1,0:T(8,128)S(1)} collective-permute-done((f32[2,128,128]{2,1,0:T(8,128)S(1)}, f32[2,128,128]{2,1,0:T(8,128)S(1)}, u32[]{:S(2)}, u32[]{:S(2)}) %collective-permute-start.5) | collective-permute-done | bytes 131104 | tf_op jit(solution)/shard_map/ppermute | solution.py:12
  133.9 3.1 %collective-permute-start.6 = (f32[2,128,128]{2,1,0:T(8,128)S(1)}, f32[2,128,128]{2,1,0:T(8,128)S(1)}, u32[]{:S(2)}, u32[]{:S(2)}) collective-permute-start(f32[2,128,128]{2,1,0:T(8,128)S(1)} %add.1281), channel_id=1, source_target_pairs={{0,64},{32,96},{64,0},{96,32},{128,192},{160,224},{192,128},{224,1... | collective-permute-start | bytes 393224 | tf_op jit(solution)/shard_map/ppermute | solution.py:12
  137.2 4.0 %collective-permute-done.6 = f32[2,128,128]{2,1,0:T(8,128)S(1)} collective-permute-done((f32[2,128,128]{2,1,0:T(8,128)S(1)}, f32[2,128,128]{2,1,0:T(8,128)S(1)}, u32[]{:S(2)}, u32[]{:S(2)}) %collective-permute-start.6) | collective-permute-done | bytes 131104 | tf_op jit(solution)/shard_map/ppermute | solution.py:12
  141.3 9.4 %collective-permute-start.7 = (f32[2,128,128]{2,1,0:T(8,128)S(1)}, f32[2,128,128]{2,1,0:T(8,128)S(1)}, u32[]{:S(2)}, u32[]{:S(2)}) collective-permute-start(f32[2,128,128]{2,1,0:T(8,128)S(1)} %add.1282), channel_id=1, source_target_pairs={{0,128},{32,160},{64,192},{96,224},{128,0},{160,32},{192,64},{224,... | collective-permute-start | bytes 393224 | tf_op jit(solution)/shard_map/ppermute | solution.py:12
  150.8 4.6 %collective-permute-done.7 = f32[2,128,128]{2,1,0:T(8,128)S(1)} collective-permute-done((f32[2,128,128]{2,1,0:T(8,128)S(1)}, f32[2,128,128]{2,1,0:T(8,128)S(1)}, u32[]{:S(2)}, u32[]{:S(2)}) %collective-permute-start.7) | collective-permute-done | bytes 131104 | tf_op jit(solution)/shard_map/ppermute | solution.py:12
  155.8 2.2 %fusion = f32[1024,2,128]{0,2,1:T(8,128)} fusion(f32[1024,2,8]{0,2,1:T(8,128)S(1)} %copy-done.35, bf16[1024,2,128,1]{2,1,0,3:T(2,128)(2,1)S(1)} %bitcast.268, bf16[8,2,128,128]{3,2,1,0:T(8,128)(2,1)S(1)} %fusion.75), kind=kOutput, calls=%fused_computation.1 | convolution fusion | flops 540803072 | bytes 2162688 | tf_op jit(solution)/shard_map/the,lhde->thld/dot_general | solution.py:156
  158.0 1.6 copy.100
  159.6 3.4 %fusion.1 = f32[1024,2,128]{0,2,1:T(8,128)} fusion(f32[1024,2,8]{0,2,1:T(8,128)S(1)} %copy-done.36, bf16[1024,2,128,1]{2,1,0,3:T(2,128)(2,1)S(1)} %bitcast.260, bf16[8,2,128,128]{3,2,1,0:T(8,128)(2,1)} %copy-done.43), kind=kOutput, calls=%fused_computation.3 | convolution fusion | flops 540803072 | bytes 2162688 | tf_op jit(solution)/shard_map/thd,lhde->thle/dot_general | solution.py:152
  163.0 1.6 copy.88
  164.6 1.2 collective-permute-done.13
  166.8 3.8 %collective-permute-start.14 = (f32[2,2,128,128]{3,2,0,1:T(8,128)S(1)}, f32[2,2,128,128]{3,2,0,1:T(8,128)S(1)}, u32[]{:S(2)}, u32[]{:S(2)}) collective-permute-start(f32[2,2,128,128]{3,2,0,1:T(8,128)S(1)} %slice_add_fusion.5), channel_id=1, source_target_pairs={{0,64},{32,96},{64,0},{96,32},{128,192},{160,224},{192,128},{224,1... | collective-permute-start | bytes 786440 | tf_op jit(solution)/shard_map/ppermute | solution.py:12
  170.5 2.3 %maximum_add_fusion.1 = f32[1024,256]{1,0:T(8,128)} fusion(f32[1024,256]{1,0:T(8,128)S(1)} %copy.100, f32[512,256]{1,0:T(8,128)} %copy.97, f32[512,256]{1,0:T(8,128)} %copy.96), kind=kLoop, calls=%fused_computation.40 | loop fusion | flops 524288 | bytes 3145728 | tf_op jit(solution)/shard_map/add | solution.py:164
  172.8 6.9 %collective-permute-done.14 = f32[2,2,128,128]{3,2,0,1:T(8,128)S(1)} collective-permute-done((f32[2,2,128,128]{3,2,0,1:T(8,128)S(1)}, f32[2,2,128,128]{3,2,0,1:T(8,128)S(1)}, u32[]{:S(2)}, u32[]{:S(2)}) %collective-permute-start.14) | collective-permute-done | bytes 262176 | tf_op jit(solution)/shard_map/ppermute | solution.py:12
  179.7 3.2 %collective-permute-start.15 = (f32[1,2,128,128]{3,2,0,1:T(8,128)S(1)}, f32[1,2,128,128]{3,2,0,1:T(8,128)S(1)}, u32[]{:S(2)}, u32[]{:S(2)}) collective-permute-start(f32[1,2,128,128]{3,2,0,1:T(8,128)S(1)} %slice_add_fusion.6), channel_id=1, source_target_pairs={{0,128},{32,160},{64,192},{96,224},{128,0},{160,32},{192,64},{224,... | collective-permute-start | bytes 393224 | tf_op jit(solution)/shard_map/ppermute | solution.py:12
  184.0 5.8 %collective-permute-done.15 = f32[1,2,128,128]{3,2,0,1:T(8,128)S(1)} collective-permute-done((f32[1,2,128,128]{3,2,0,1:T(8,128)S(1)}, f32[1,2,128,128]{3,2,0,1:T(8,128)S(1)}, u32[]{:S(2)}, u32[]{:S(2)}) %collective-permute-start.15) | collective-permute-done | bytes 131104 | tf_op jit(solution)/shard_map/ppermute | solution.py:12
  189.8 1.3 fusion.53
  191.5 1.3 copy.107
  193.1 1.3 copy.106
  (169 shorter events, 28.0 us)
Async XLA Ops:
  0.6 3.5 %copy-start.17 = (bf16[1024,256]{1,0:T(8,128)(2,1)S(1)}, bf16[1024,256]{1,0:T(8,128)(2,1)}, u32[]{:S(2)}) copy-start(bf16[1024,256]{1,0:T(8,128)(2,1)} %param.21) | copy-start | bytes 1572868
  2.4 2.0 %copy-start.34 = (f32[1024,2,8]{0,2,1:T(8,128)}, f32[1024,2,8]{0,2,1:T(8,128)S(1)}, u32[]{:S(2)}) copy-start(f32[1024,2,8]{0,2,1:T(8,128)S(1)} %slice.350) | copy-start | bytes 196612
  5.2 2.2 %copy-start = (bf16[1024,256]{1,0:T(8,128)(2,1)S(1)}, bf16[1024,256]{1,0:T(8,128)(2,1)}, u32[]{:S(2)}) copy-start(bf16[1024,256]{1,0:T(8,128)(2,1)} %param.19) | copy-start | bytes 1572868
  5.2 2.5 %copy-start.2 = (bf16[1024,256]{1,0:T(8,128)(2,1)S(1)}, bf16[1024,256]{1,0:T(8,128)(2,1)}, u32[]{:S(2)}) copy-start(bf16[1024,256]{1,0:T(8,128)(2,1)} %param.20) | copy-start | bytes 1572868
  7.4 2.4 %copy-start.16 = (bf16[1024,256]{1,0:T(8,128)(2,1)S(1)}, bf16[1024,256]{1,0:T(8,128)(2,1)}, u32[]{:S(2)}) copy-start(bf16[1024,256]{1,0:T(8,128)(2,1)} %param.18) | copy-start | bytes 1572868
  7.4 43.9 %collective-permute-start.8 = (f32[8,2,128,128]{3,2,0,1:T(8,128)}, f32[8,2,128,128]{3,2,0,1:T(8,128)}, u32[]{:S(2)}, u32[]{:S(2)}) collective-permute-start(f32[8,2,128,128]{3,2,0,1:T(8,128)} %fusion.19), channel_id=1, source_target_pairs={{0,1},{1,0},{2,3},{3,2},{4,5},{5,4},{6,7},{7,6},{8,9},{9,8},{10,11... | collective-permute-start | bytes 3145736 | tf_op jit(solution)/shard_map/ppermute | solution.py:12
  7.7 8.2 %copy-start.20 = (bf16[1024,256]{0,1:T(8,128)(2,1)}, bf16[1024,256]{0,1:T(8,128)(2,1)S(1)}, u32[]{:S(2)}) copy-start(bf16[1024,256]{0,1:T(8,128)(2,1)S(1)} %copy.211) | copy-start | bytes 1572868
  8.6 75.3 %collective-permute-start = (f32[2,128,128]{2,1,0:T(8,128)}, f32[2,128,128]{2,1,0:T(8,128)S(1)}, u32[]{:S(2)}, u32[]{:S(2)}) collective-permute-start(f32[2,128,128]{2,1,0:T(8,128)} %fusion.34), channel_id=1, source_target_pairs={{0,1},{1,0},{2,3},{3,2},{4,5},{5,4},{6,7},{7,6},{8,9},{9,8},{10,11... | collective-permute-start | bytes 393224 | tf_op jit(solution)/shard_map/ppermute | solution.py:12
  18.9 7.7 %copy-start.28 = (bf16[512,256]{1,0:T(8,128)(2,1)S(1)}, bf16[512,256]{1,0:T(8,128)(2,1)}, u32[]{:S(2)}) copy-start(bf16[512,256]{1,0:T(8,128)(2,1)} %get-tuple-element.83) | copy-start | bytes 786436
  18.9 7.9 %copy-start.27 = (bf16[512,256]{1,0:T(8,128)(2,1)S(1)}, bf16[512,256]{1,0:T(8,128)(2,1)}, u32[]{:S(2)}) copy-start(bf16[512,256]{1,0:T(8,128)(2,1)} %get-tuple-element.82) | copy-start | bytes 786436
  18.9 8.0 %slice-start = ((bf16[1024,256]{1,0:T(8,128)(2,1)}), bf16[512,256]{1,0:T(8,128)(2,1)S(1)}, s32[]{:S(2)}) async-start(bf16[1024,256]{1,0:T(8,128)(2,1)} %param.19), calls=%async_computation | async-start | bytes 524288 | tf_op jit(solution)/shard_map/slice | solution.py:92
  26.6 1.7 slice-start.1
  26.6 6.1 %copy-start.25 = (pred[512,512]{1,0:T(8,128)(4,1)S(1)}, pred[512,512]{1,0:T(8,128)(4,1)}, u32[]{:S(2)}) copy-start(pred[512,512]{1,0:T(8,128)(4,1)} %get-tuple-element.138) | copy-start | bytes 786436
  26.6 6.1 %copy-start.26 = (pred[512,512]{1,0:T(8,128)(4,1)S(1)}, pred[512,512]{1,0:T(8,128)(4,1)}, u32[]{:S(2)}) copy-start(pred[512,512]{1,0:T(8,128)(4,1)} %get-tuple-element.139) | copy-start | bytes 786436
  38.2 1.6 copy-start.10
  38.2 1.8 copy-start.11
  38.3 1.9 copy-start.12
  38.3 2.1 %copy-start.13 = (pred[512,1024]{1,0:T(8,128)(4,1)S(1)}, pred[512,1024]{1,0:T(8,128)(4,1)}, u32[]{:S(2)}) copy-start(pred[512,1024]{1,0:T(8,128)(4,1)} %get-tuple-element.115) | copy-start | bytes 1572868
  38.3 2.2 %copy-start.14 = (pred[512,1024]{1,0:T(8,128)(4,1)S(1)}, pred[512,1024]{1,0:T(8,128)(4,1)}, u32[]{:S(2)}) copy-start(pred[512,1024]{1,0:T(8,128)(4,1)} %get-tuple-element.116) | copy-start | bytes 1572868
  38.3 2.4 %copy-start.15 = (pred[512,1024]{1,0:T(8,128)(4,1)S(1)}, pred[512,1024]{1,0:T(8,128)(4,1)}, u32[]{:S(2)}) copy-start(pred[512,1024]{1,0:T(8,128)(4,1)} %get-tuple-element.117) | copy-start | bytes 1572868
  40.7 7.2 %copy-start.3 = (bf16[1024,256]{1,0:T(8,128)(2,1)S(1)}, bf16[1024,256]{1,0:T(8,128)(2,1)}, u32[]{:S(2)}) copy-start(bf16[1024,256]{1,0:T(8,128)(2,1)} %param.20) | copy-start | bytes 1572868
  52.9 22.8 %collective-permute-start.9 = (f32[7,2,128,128]{3,2,0,1:T(8,128)S(1)}, f32[7,2,128,128]{3,2,0,1:T(8,128)S(1)}, u32[]{:S(2)}, u32[]{:S(2)}) collective-permute-start(f32[7,2,128,128]{3,2,0,1:T(8,128)S(1)} %slice_add_fusion), channel_id=1, source_target_pairs={{0,2},{1,3},{2,0},{3,1},{4,6},{5,7},{6,4},{7,5},{8,10},{9,11},{10,... | collective-permute-start | bytes 2752520 | tf_op jit(solution)/shard_map/ppermute | solution.py:12
  75.7 2.5 %copy-start.29 = (f32[7,2,128,128]{3,2,0,1:T(8,128)}, f32[7,2,128,128]{3,2,0,1:T(8,128)S(1)}, u32[]{:S(2)}) copy-start(f32[7,2,128,128]{3,2,0,1:T(8,128)S(1)} %collective-permute-done.9) | copy-start | bytes 2752516
  75.8 31.0 %collective-permute-start.10 = (f32[6,2,128,128]{3,2,0,1:T(8,128)S(1)}, f32[6,2,128,128]{3,2,0,1:T(8,128)}, u32[]{:S(2)}, u32[]{:S(2)}) collective-permute-start(f32[6,2,128,128]{3,2,0,1:T(8,128)S(1)} %slice_add_fusion.1), channel_id=1, source_target_pairs={{0,4},{1,5},{2,6},{3,7},{4,0},{5,1},{6,2},{7,3},{8,12},{9,13},{10,... | collective-permute-start | bytes 2359304 | tf_op jit(solution)/shard_map/ppermute | solution.py:12
  78.7 3.2 %copy-start.24 = (f32[2,512,128]{1,2,0:T(8,128)S(1)}, f32[2,512,128]{1,2,0:T(8,128)}, u32[]{:S(2)}) copy-start(f32[2,512,128]{1,2,0:T(8,128)} %fusion.30) | copy-start | bytes 1572868
  84.9 13.7 %collective-permute-start.1 = (f32[2,128,128]{2,1,0:T(8,128)S(1)}, f32[2,128,128]{2,1,0:T(8,128)S(1)}, u32[]{:S(2)}, u32[]{:S(2)}) collective-permute-start(f32[2,128,128]{2,1,0:T(8,128)S(1)} %add.1276), channel_id=1, source_target_pairs={{0,2},{1,3},{2,0},{3,1},{4,6},{5,7},{6,4},{7,5},{8,10},{9,11},{10,... | collective-permute-start | bytes 393224 | tf_op jit(solution)/shard_map/ppermute | solution.py:12
  98.6 6.6 %collective-permute-start.2 = (f32[2,128,128]{2,1,0:T(8,128)S(1)}, f32[2,128,128]{2,1,0:T(8,128)S(1)}, u32[]{:S(2)}, u32[]{:S(2)}) collective-permute-start(f32[2,128,128]{2,1,0:T(8,128)S(1)} %add.1277), channel_id=1, source_target_pairs={{0,4},{1,5},{2,6},{3,7},{4,0},{5,1},{6,2},{7,3},{8,12},{9,13},{10,... | collective-permute-start | bytes 393224 | tf_op jit(solution)/shard_map/ppermute | solution.py:12
  105.2 6.5 %collective-permute-start.3 = (f32[2,128,128]{2,1,0:T(8,128)S(1)}, f32[2,128,128]{2,1,0:T(8,128)S(1)}, u32[]{:S(2)}, u32[]{:S(2)}) collective-permute-start(f32[2,128,128]{2,1,0:T(8,128)S(1)} %add.1278), channel_id=1, source_target_pairs={{0,8},{1,9},{2,10},{3,11},{4,12},{5,13},{6,14},{7,15},{8,0},{9,1},... | collective-permute-start | bytes 393224 | tf_op jit(solution)/shard_map/ppermute | solution.py:12
  108.0 28.9 %collective-permute-start.11 = (f32[5,2,128,128]{3,2,0,1:T(8,128)S(1)}, f32[5,2,128,128]{3,2,0,1:T(8,128)S(1)}, u32[]{:S(2)}, u32[]{:S(2)}) collective-permute-start(f32[5,2,128,128]{3,2,0,1:T(8,128)S(1)} %slice_add_fusion.2), channel_id=1, source_target_pairs={{0,8},{1,9},{2,10},{3,11},{4,12},{5,13},{6,14},{7,15},{8,0},{9,1},... | collective-permute-start | bytes 1966088 | tf_op jit(solution)/shard_map/ppermute | solution.py:12
  111.6 15.9 %collective-permute-start.4 = (f32[2,128,128]{2,1,0:T(8,128)S(1)}, f32[2,128,128]{2,1,0:T(8,128)S(1)}, u32[]{:S(2)}, u32[]{:S(2)}) collective-permute-start(f32[2,128,128]{2,1,0:T(8,128)S(1)} %add.1279), channel_id=1, source_target_pairs={{0,16},{1,17},{2,18},{3,19},{4,20},{5,21},{6,22},{7,23},{8,24},{9,... | collective-permute-start | bytes 393224 | tf_op jit(solution)/shard_map/ppermute | solution.py:12
  127.5 6.3 %collective-permute-start.5 = (f32[2,128,128]{2,1,0:T(8,128)S(1)}, f32[2,128,128]{2,1,0:T(8,128)S(1)}, u32[]{:S(2)}, u32[]{:S(2)}) collective-permute-start(f32[2,128,128]{2,1,0:T(8,128)S(1)} %add.1280), channel_id=1, source_target_pairs={{0,32},{32,0},{64,96},{96,64},{128,160},{160,128},{192,224},{224,1... | collective-permute-start | bytes 393224 | tf_op jit(solution)/shard_map/ppermute | solution.py:12
  129.6 26.2 %copy-start.32 = (bf16[1024,2,128]{2,1,0:T(2,128)(2,1)S(1)}, bf16[1024,2,128]{2,1,0:T(2,128)(2,1)}, u32[]{:S(2)}) copy-start(bf16[1024,2,128]{2,1,0:T(2,128)(2,1)} %copy-done.31) | copy-start | bytes 1572868
  129.6 26.2 %copy-start.35 = (f32[1024,2,8]{0,2,1:T(8,128)S(1)}, f32[1024,2,8]{0,2,1:T(8,128)}, u32[]{:S(2)}) copy-start(f32[1024,2,8]{0,2,1:T(8,128)} %copy-done.34) | copy-start | bytes 196612
  133.9 7.4 %collective-permute-start.6 = (f32[2,128,128]{2,1,0:T(8,128)S(1)}, f32[2,128,128]{2,1,0:T(8,128)S(1)}, u32[]{:S(2)}, u32[]{:S(2)}) collective-permute-start(f32[2,128,128]{2,1,0:T(8,128)S(1)} %add.1281), channel_id=1, source_target_pairs={{0,64},{32,96},{64,0},{96,32},{128,192},{160,224},{192,128},{224,1... | collective-permute-start | bytes 393224 | tf_op jit(solution)/shard_map/ppermute | solution.py:12
  136.9 18.5 %copy-start.30 = (f32[5,2,128,128]{3,2,0,1:T(8,128)}, f32[5,2,128,128]{3,2,0,1:T(8,128)S(1)}, u32[]{:S(2)}) copy-start(f32[5,2,128,128]{3,2,0,1:T(8,128)S(1)} %collective-permute-done.11) | copy-start | bytes 1966084
  137.0 18.4 %collective-permute-start.12 = (f32[4,2,128,128]{3,2,0,1:T(8,128)S(1)}, f32[4,2,128,128]{3,2,0,1:T(8,128)S(1)}, u32[]{:S(2)}, u32[]{:S(2)}) collective-permute-start(f32[4,2,128,128]{3,2,0,1:T(8,128)S(1)} %slice_add_fusion.3), channel_id=1, source_target_pairs={{0,16},{1,17},{2,18},{3,19},{4,20},{5,21},{6,22},{7,23},{8,24},{9,... | collective-permute-start | bytes 1572872 | tf_op jit(solution)/shard_map/ppermute | solution.py:12
  141.3 14.0 %collective-permute-start.7 = (f32[2,128,128]{2,1,0:T(8,128)S(1)}, f32[2,128,128]{2,1,0:T(8,128)S(1)}, u32[]{:S(2)}, u32[]{:S(2)}) collective-permute-start(f32[2,128,128]{2,1,0:T(8,128)S(1)} %add.1282), channel_id=1, source_target_pairs={{0,128},{32,160},{64,192},{96,224},{128,0},{160,32},{192,64},{224,... | collective-permute-start | bytes 393224 | tf_op jit(solution)/shard_map/ppermute | solution.py:12
  155.4 2.6 %copy-start.43 = (bf16[8,2,128,128]{3,2,1,0:T(8,128)(2,1)}, bf16[8,2,128,128]{3,2,1,0:T(8,128)(2,1)S(1)}, u32[]{:S(2)}) copy-start(bf16[8,2,128,128]{3,2,1,0:T(8,128)(2,1)S(1)} %fusion.75) | copy-start | bytes 1572868
  155.4 2.6 %copy-start.33 = (f32[4,2,128,128]{3,2,0,1:T(8,128)}, f32[4,2,128,128]{3,2,0,1:T(8,128)S(1)}, u32[]{:S(2)}) copy-start(f32[4,2,128,128]{3,2,0,1:T(8,128)S(1)} %collective-permute-done.12) | copy-start | bytes 1572868
  155.5 10.3 %collective-permute-start.13 = (f32[3,2,128,128]{3,2,0,1:T(8,128)S(1)}, f32[3,2,128,128]{3,2,0,1:T(8,128)}, u32[]{:S(2)}, u32[]{:S(2)}) collective-permute-start(f32[3,2,128,128]{3,2,0,1:T(8,128)S(1)} %slice_add_fusion.4), channel_id=1, source_target_pairs={{0,32},{32,0},{64,96},{96,64},{128,160},{160,128},{192,224},{224,1... | collective-permute-start | bytes 1179656 | tf_op jit(solution)/shard_map/ppermute | solution.py:12
  158.0 1.6 copy-start.19
  158.0 1.6 copy-start.36
  164.6 18.3 %copy-start.22 = (f32[512,256]{1,0:T(8,128)S(1)}, f32[512,256]{1,0:T(8,128)}, u32[]{:S(2)}) copy-start(f32[512,256]{1,0:T(8,128)} %copy.83) | copy-start | bytes 1572868
  164.6 18.3 %copy-start.23 = (f32[512,256]{1,0:T(8,128)S(1)}, f32[512,256]{1,0:T(8,128)}, u32[]{:S(2)}) copy-start(f32[512,256]{1,0:T(8,128)} %copy.82) | copy-start | bytes 1572868
  166.8 12.9 %collective-permute-start.14 = (f32[2,2,128,128]{3,2,0,1:T(8,128)S(1)}, f32[2,2,128,128]{3,2,0,1:T(8,128)S(1)}, u32[]{:S(2)}, u32[]{:S(2)}) collective-permute-start(f32[2,2,128,128]{3,2,0,1:T(8,128)S(1)} %slice_add_fusion.5), channel_id=1, source_target_pairs={{0,64},{32,96},{64,0},{96,32},{128,192},{160,224},{192,128},{224,1... | collective-permute-start | bytes 786440 | tf_op jit(solution)/shard_map/ppermute | solution.py:12
  179.7 11.4 %copy-start.4 = (f32[1024,2,128]{0,2,1:T(8,128)S(1)}, f32[1024,2,128]{0,2,1:T(8,128)}, u32[]{:S(2)}) copy-start(f32[1024,2,128]{0,2,1:T(8,128)} %fusion.18) | copy-start | bytes 3145732
  179.7 10.1 %collective-permute-start.15 = (f32[1,2,128,128]{3,2,0,1:T(8,128)S(1)}, f32[1,2,128,128]{3,2,0,1:T(8,128)S(1)}, u32[]{:S(2)}, u32[]{:S(2)}) collective-permute-start(f32[1,2,128,128]{3,2,0,1:T(8,128)S(1)} %slice_add_fusion.6), channel_id=1, source_target_pairs={{0,128},{32,160},{64,192},{96,224},{128,0},{160,32},{192,64},{224,... | collective-permute-start | bytes 393224 | tf_op jit(solution)/shard_map/ppermute | solution.py:12
  191.1 1.7 copy-start.5
  (14 other events, 15.2 us)
where the time goes:
time: 195 us; the launch traced here: 194 us
  waiting for transfers between devices  75.3 us (39%)
  other arithmetic  36.4 us (19%)
  starting transfers between devices  35.4 us (18%)
  local copies, waits for them, and re-layouts  25.3 us (13%)
  matrix products  20.6 us (11%)
    ppermute x16, waiting for transfers between devices, from_partner(): lax.ppermute(x, axis, [(i, i ^ 1 << distance) for i in range(lax.axis_siz...  75.3 us
    ppermute x16, starting transfers between devices, from_partner(): lax.ppermute(x, axis, [(i, i ^ 1 << distance) for i in range(lax.axis_siz...  35.4 us
    select_n x2, other arithmetic, local_attention(): level_mask = jnp.where(causal[None], level_mask, 0.0)  11.8 us
    le x2, other arithmetic, local_attention(): causal = col_places[None, :] <= row_places[:, None]  8.8 us
    unnamed x96, local copies, waits for them, and re-layouts  7.82 us
    eq x5, other arithmetic, local_attention(): levels[None] == level  5.83 us
    transpose x11, local copies, waits for them, and re-layouts, local_attention(): jnp.transpose(block_weights[:, :, level])[:, :, None]  4.21 us
    add x7, other arithmetic, fenwick_states(): stacked = stacked[1:] + other_stack[1:]  3.93 us
  transfers between devices with their start and end apart: 16, of which 11 were waited for; matrix products, arithmetic and copies ran while one was open for 35% of the time, Pallas kernels for 0%

commit v1 on v0

v1 whole, which is shorter than its diff:
```python
import functools
import math

import jax
import jax.numpy as jnp
from jax import lax
from jax.experimental import pallas as pl
from jax.experimental.pallas import tpu as pltpu
from jax.sharding import PartitionSpec as P

F32 = jnp.float32
BF16 = jnp.bfloat16
AXES = ("col", "row")
BLOCK = 256
SMALL = 128


def contract(a, b, dim_a, dim_b):
    return lax.dot_general(
        a, b, (((dim_a,), (dim_b,)), ((), ())), preferred_element_type=F32
    )


def level_weights(table, profile_row, width):
    profiles, levels = table.shape
    places = lax.broadcasted_iota(jnp.int32, (profiles, profile_row.shape[1]), 0)
    onehot = jnp.where(places == profile_row, 1.0, 0.0).astype(BF16)
    high = table.astype(BF16)
    rest = table - high.astype(F32)
    middle = rest.astype(BF16)
    low = (rest - middle.astype(F32)).astype(BF16)
    picked = (contract(onehot, high, 0, 0) + contract(onehot, middle, 0, 0)) + contract(
        onehot, low, 0, 0
    )
    depth = lax.broadcasted_iota(jnp.int32, (1, levels), 1).astype(F32)
    return picked * (jnp.exp2(-0.5 * depth) / math.sqrt(width))


def weighted_stack(q, w, levels):
    q_wide = q.astype(F32)
    return jnp.concatenate([(q_wide * w[:, l : l + 1]).astype(BF16) for l in levels], axis=1)


def first_kernel(first_far, width, heads, ends, profile, table, q, k, v, g, w_out, s_out, g_out):
    for h in range(heads):
        lanes = slice(h * width, (h + 1) * width)
        w = level_weights(table[:, h, :], profile[...], width)
        w_out[h] = w
        s_out[h] = contract(k[:, lanes], v[:, lanes], 0, 0)
        stack = weighted_stack(q[:, lanes], w, [first_far + j for j in ends])
        states = contract(g[:, lanes], stack, 0, 0)
        for i in range(len(ends)):
            g_out[i, h] = states[:, i * width : (i + 1) * width]


def second_kernel(first_far, width, heads, middle, w_in, q, g, g_out):
    for h in range(heads):
        lanes = slice(h * width, (h + 1) * width)
        stack = weighted_stack(q[:, lanes], w_in[h], [first_far + j for j in middle])
        states = contract(g[:, lanes], stack, 0, 0)
        for i in range(len(middle)):
            g_out[i, h] = states[:, i * width : (i + 1) * width]


def block_mask(w, levels, causal):
    parts = []
    for i in range(BLOCK // SMALL):
        rows = w[i * SMALL : (i + 1) * SMALL]
        tri = jnp.broadcast_to(rows[:, 0:1], (SMALL, SMALL))
        for l in range(1, SMALL.bit_length()):
            tri = jnp.where(levels >= l, rows[:, l : l + 1], tri)
        line = []
        for j in range(BLOCK // SMALL):
            if j > i:
                line.append(jnp.zeros((SMALL, SMALL), F32))
            elif j == i:
                line.append(jnp.where(causal, tri, 0.0))
            else:
                l = SMALL.bit_length() - 1 + (i ^ j).bit_length()
                line.append(jnp.broadcast_to(rows[:, l : l + 1], (SMALL, SMALL)))
        parts.append(jnp.concatenate(line, axis=1))
    return jnp.concatenate(parts, axis=0)


def tile_kernel(w_in, q, k, v, g, out, dq, dk, dv):
    tokens = q.shape[0]
    places_t = lax.broadcasted_iota(jnp.int32, (SMALL, SMALL), 0)
    places_s = lax.broadcasted_iota(jnp.int32, (SMALL, SMALL), 1)
    differ = places_t ^ places_s
    levels = jnp.zeros((SMALL, SMALL), jnp.int32)
    for p in range(SMALL.bit_length() - 1):
        levels = levels + jnp.where(differ >= 1 << p, 1, 0)
    causal = places_s <= places_t
    for start in range(0, tokens, BLOCK):
        rows = slice(start, start + BLOCK)
        qb, kb, vb, gb = q[rows, :], k[rows, :], v[rows, :], g[rows, :]
        mask = block_mask(w_in[0, rows, :], levels, causal)
        probs = (contract(qb, kb, 1, 1) * mask).astype(BF16)
        grads = (contract(gb, vb, 1, 1) * mask).astype(BF16)
        out[rows, :] = contract(probs, vb, 1, 0)
        dq[rows, :] = contract(grads, kb, 1, 0)
        dk[rows, :] = contract(grads, qb, 0, 0)
        dv[rows, :] = contract(probs, gb, 0, 0)
    size = BLOCK
    while size < tokens:
        l = size.bit_length()
        for start in range(0, tokens, 2 * size):
            low = slice(start, start + size)
            up = slice(start + size, start + 2 * size)
            w = w_in[0, up, l : l + 1]
            state = contract(k[low, :], v[low, :], 0, 0).astype(BF16)
            out[up, :] = out[up, :] + w * contract(q[up, :], state, 1, 0)
            dq[up, :] = dq[up, :] + w * contract(g[up, :], state, 1, 1)
            weighted = (q[up, :].astype(F32) * w).astype(BF16)
            pulled = contract(g[up, :], weighted, 0, 0).astype(BF16)
            dk[low, :] = dk[low, :] + contract(v[low, :], pulled, 1, 0)
            dv[low, :] = dv[low, :] + contract(k[low, :], pulled, 1, 1)
        size *= 2


def far_sums(first, width, h, w_in, q, g, buckets, count):
    lanes = slice(h * width, (h + 1) * width)
    qh, gh = q[:, lanes], g[:, lanes]
    out = dq = None
    for i in range(count):
        state = buckets[i, h].astype(BF16)
        w = w_in[h, :, first + i : first + i + 1]
        o = w * contract(qh, state, 1, 0)
        d = w * contract(gh, state, 1, 1)
        out, dq = (o, d) if out is None else (out + o, dq + d)
    return out, dq


def far_kernel(first, width, heads, count, w_in, q, g, buckets, out, dq):
    for h in range(heads):
        lanes = slice(h * width, (h + 1) * width)
        out[:, lanes], dq[:, lanes] = far_sums(first, width, h, w_in, q, g, buckets, count)


def last_kernel(first, width, heads, count, w_in, q, k, v, g, buckets, pulled, far_out, far_dq, *refs):
    local, (out, dq, dk, dv) = refs[:-4], refs[-4:]
    for h in range(heads):
        lanes = slice(h * width, (h + 1) * width)
        o, d = far_sums(first, width, h, w_in, q, g, buckets, count)
        l_out, l_dq, l_dk, l_dv = local[4 * h : 4 * h + 4]
        state = pulled[h].astype(BF16)
        out[:, lanes] = l_out[...] + (far_out[:, lanes] + o)
        dq[:, lanes] = l_dq[...] + (far_dq[:, lanes] + d)
        dk[:, lanes] = l_dk[...] + contract(v[:, lanes], state, 1, 0)
        dv[:, lanes] = l_dv[...] + contract(k[:, lanes], state, 1, 1)


def links(row_bits, col_bits):
    steps = []
    place = 1
    while place < row_bits:
        steps.append(1 << place)
        if place + 1 < row_bits:
            steps.append(3 << place)
        place += 2
    for bit in range(col_bits):
        if bit == col_bits - 1 and bit > 0:
            steps.append(((1 << col_bits) - 1) << row_bits)
        else:
            steps.append(1 << row_bits + bit)
    return steps


def tie(*trees):
    return lax.optimization_barrier(trees)


def shards(row_size, col_size, queries, keys, values, out_grad, weight_table, profile):
    tokens, columns = queries.shape
    profiles, heads, depth = weight_table.shape
    width = columns // heads
    row_bits = row_size.bit_length() - 1
    col_bits = col_size.bit_length() - 1
    far = row_bits + col_bits
    first_far = tokens.bit_length()
    devices = row_size * col_size
    own = lax.axis_index("col") * row_size + lax.axis_index("row")
    core = own & 1
    on_first = core == 0
    profile_row = profile.reshape(1, tokens)

    def full(shape, kind=F32):
        return jax.ShapeDtypeStruct(shape, kind)

    square = (heads, width, width)
    ends = (far - 1, 0)
    middle = tuple(range(1, far - 1))
    unit = tokens * width * width * heads * 2
    weights, state, end_grads = pl.pallas_call(
        functools.partial(first_kernel, first_far, width, heads, ends),
        out_shape=(full((heads, tokens, depth)), full(square), full((2,) + square)),
        name="first",
        cost_estimate=pl.CostEstimate(
            flops=3 * unit, bytes_accessed=4 * tokens * columns * 2, transcendentals=0
        ),
    )(profile_row, weight_table, queries, keys, values, out_grad)

    exchange = [(i, i ^ 1) for i in range(devices)]
    hand_over = [(i, i ^ 1) for i in range(0, devices, 2)]
    payload = jnp.stack([state, jnp.where(on_first, end_grads[0], end_grads[1])])
    other = lax.ppermute(payload, AXES, exchange)
    middle_grads = pl.pallas_call(
        functools.partial(second_kernel, first_far, width, heads, middle),
        out_shape=full((len(middle),) + square),
        name="second",
        cost_estimate=pl.CostEstimate(
            flops=len(middle) * unit, bytes_accessed=tokens * columns * 4, transcendentals=0
        ),
    )(weights, queries, out_grad)
    other_middle = lax.ppermute(middle_grads, AXES, hand_over)

    steps = links(row_bits, col_bits)
    rounds = len(steps)
    carried = jnp.where(on_first, state + other[0], 0.0)
    received = []

    def tile_part(h):
        block = pl.BlockSpec((tokens, width), lambda i: (0, h))
        whole = pl.BlockSpec((tokens, width), lambda i: (0, 0))

        def run(w, q, k, v, g):
            return pl.pallas_call(
                tile_kernel,
                grid=(1,),
                in_specs=[pl.BlockSpec((1, tokens, depth), lambda i: (h, 0, 0))] + [block] * 4,
                out_specs=[whole] * 4,
                out_shape=[full((tokens, width))] * 4,
                name=f"tile{h}",
                cost_estimate=pl.CostEstimate(
                    flops=12 * tokens * BLOCK * width,
                    bytes_accessed=tokens * width * 24,
                    transcendentals=0,
                ),
            )(w, q, k, v, g)

        return run

    early = 5

    def early_far(w, q, g, buckets):
        return pl.pallas_call(
            functools.partial(far_kernel, first_far, width, heads, early),
            out_shape=[full((tokens, columns))] * 2,
            name="far",
            cost_estimate=pl.CostEstimate(
                flops=2 * early * unit, bytes_accessed=tokens * columns * 12, transcendentals=0
            ),
        )(w, q, g, buckets)

    local = {}
    for r in range(1, rounds + 1):
        level = far - r
        is_upper = (core == 1) & ((own >> level & 1) == 1)
        own_part = end_grads[0] if level == far - 1 else middle_grads[level - 1]
        from_other = other[1] if level == far - 1 else other_middle[level - 1]
        send = carried + jnp.where(is_upper, own_part + from_other, 0.0)
        pairs = [
            (i, i ^ (steps[rounds - r] if i & 1 else steps[r - 1])) for i in range(devices)
        ]
        work = None
        if r <= heads:
            work, operands = tile_part(r - 1), (weights, queries, keys, values, out_grad)
        if r == rounds - 1:
            taken = []
            for l in range(early):
                if l == 0:
                    here = jnp.where(on_first, 0.0, other[0])
                else:
                    here = jnp.where(on_first, received[l - 1], handed[l - 1])
                    here = jnp.where((own >> l & 1) == 1, here, 0.0)
                taken.append(here)
            work, operands = early_far, (weights, queries, out_grad, jnp.stack(taken))
        if work is not None:
            send, operands = tie(send, operands)
        got = lax.ppermute(send, AXES, pairs)
        if work is not None:
            result = work(*operands)
            got, result = tie(got, result)
            local[r] = result
        received.append(got)
        carried = carried + got
        if r == early - 1:
            handed = lax.ppermute(jnp.stack(received), AXES, hand_over)

    late = far - early
    payload = jnp.stack(
        [jnp.where(on_first, received[early - 1], carried)] + received[early:]
    )
    final = lax.ppermute(payload, AXES, exchange)
    buckets = []
    for i in range(late):
        here = jnp.where(on_first, received[early - 1 + i], final[i])
        buckets.append(jnp.where((own >> early + i & 1) == 1, here, 0.0))
    pulled = jnp.where(on_first, final[0] + other[1], carried)

    far_out, far_dq = local[rounds - 1]
    span = min(tokens, 256)
    wide = pl.BlockSpec((span, columns), lambda i: (i, 0))
    narrow = pl.BlockSpec((span, width), lambda i: (i, 0))
    return pl.pallas_call(
        functools.partial(last_kernel, first_far + early, width, heads, late),
        grid=(tokens // span,),
        in_specs=[pl.BlockSpec((heads, span, depth), lambda i: (0, i, 0))]
        + [wide] * 4
        + [
            pl.BlockSpec((late,) + square, lambda i: (0, 0, 0, 0)),
            pl.BlockSpec(square, lambda i: (0, 0, 0)),
        ]
        + [wide] * 2
        + [narrow] * (4 * heads),
        out_specs=[wide] * 4,
        out_shape=[full((tokens, columns))] * 4,
        name="last",
        cost_estimate=pl.CostEstimate(
            flops=(2 * late + 2) * unit, bytes_accessed=tokens * columns * 40, transcendentals=0
        ),
    )(
        weights,
        queries,
        keys,
        values,
        out_grad,
        jnp.stack(buckets),
        pulled,
        far_out,
        far_dq,
        *[part for h in range(heads) for part in local[h + 1]],
    )


def solution(mesh):
    spread = P(AXES, None)
    body = functools.partial(shards, mesh.shape["row"], mesh.shape["col"])
    return jax.shard_map(
        body,
        mesh=mesh,
        in_specs=(spread,) * 4 + (P(), P(AXES)),
        out_specs=(spread,) * 4,
        check_vma=False,
    )
```

time: 195 us -> 78.2 us (0.40)
  the two profiles are of different devices: /device:TPU:2 before, /device:TPU:1 now
where the time goes in v1:
time: 78.2 us; the launch traced here: 77.8 us
  Pallas kernels  32.1 us (41%)
  starting transfers between devices  24.3 us (31%)
  waiting for transfers between devices  16.1 us (21%)
  local copies, waits for them, and re-layouts  2.34 us (3%)
  other arithmetic  1.97 us (3%)
  between operations  0.96 us (1%)
    ppermute x7, waiting for transfers between devices, shards(): got = lax.ppermute(send, AXES, pairs)  13.5 us
    ppermute x7, starting transfers between devices, shards(): got = lax.ppermute(send, AXES, pairs)  12.7 us
    pallas_call x2, Pallas kernels, run(): pl.pallas_call(tile_kernel, grid=(1,), in_specs=[pl.BlockSpec((1, tokens,...  12.1 us
    pallas_call x1, Pallas kernels, shards(): pl.pallas_call(functools.partial(last_kernel, first_far + early, width, h...  6.73 us
    ppermute x1, starting transfers between devices, shards(): final = lax.ppermute(payload, AXES, exchange)  5.73 us
    pallas_call x1, Pallas kernels, early_far(): pl.pallas_call(functools.partial(far_kernel, first_far, width, heads, ear...  4.73 us
    pallas_call x1, Pallas kernels, shards(): pl.pallas_call(functools.partial(second_kernel, first_far, width, heads,...  4.46 us
    pallas_call x1, Pallas kernels, shards(): pl.pallas_call(functools.partial(first_kernel, first_far, width, heads, e...  4.11 us
  transfers between devices with their start and end apart: 11, of which 6 were waited for; matrix products, arithmetic and copies ran while one was open for 0% of the time, Pallas kernels for 22%

profile of v1, /device:TPU:1, one launch (start us, length us, event | category | flops | bytes accessed | tf_op | source)
XLA Modules:
  0.0 77.8 jit_solution(3975634691662789140)
XLA Ops:
  0.6 1.5 %copy.10.table = f32[64,2,21]{2,1,0:T(2,128)} copy(f32[64,2,21]{0,1,2:T(2,128)} %param.10) | data formatting | bytes 21504 | tf_op args[4]
  2.1 4.1 %first.1 = (f32[2,1024,21]{2,1,0:T(8,128)}, f32[2,128,128]{2,1,0:T(8,128)}, f32[2,2,128,128]{3,2,1,0:T(8,128)}) custom-call(s32[1,1024]{1,0:T(1,128)} %bitcast.146, f32[64,2,21]{2,1,0:T(2,128)} %copy.10.table, bf16[1024,256]{1,0:T(8,128)(2,1)} %q.8, bf16[1024,256]{1,0:T(8,128)(2,1)} %k.5, bf16[1024,256]{1,0:T(8,128)(2,1)} %v.5, bf16[1024,256]{1,0:T(8,128)(2,1)} %g.8), custom_call_target="tpu_custom_call" | custom-call | flops 201326592 | bytes 2097152 | tf_op jit(solution)/shard_map/first/pallas_call | solution.py:194
  6.2 0.0 copy-start.3
  6.2 4.5 %second.1 = f32[6,2,128,128]{3,2,1,0:T(8,128)} custom-call(f32[2,1024,21]{2,1,0:T(8,128)} %get-tuple-element.73.w_in, bf16[1024,256]{1,0:T(8,128)(2,1)} %q.8, bf16[1024,256]{1,0:T(8,128)(2,1)} %g.8), custom_call_target="tpu_custom_call" | custom-call | flops 402653184 | bytes 1048576 | tf_op jit(solution)/shard_map/second/pallas_call | solution.py:207
  10.7 1.3 %collective-permute-start.2 = (f32[6,2,128,128]{3,2,1,0:T(8,128)}, f32[6,2,128,128]{3,2,1,0:T(8,128)S(1)}, u32[]{:S(2)}, u32[]{:S(2)}) collective-permute-start(f32[6,2,128,128]{3,2,1,0:T(8,128)} %second.1), channel_id=1, source_target_pairs={{0,1},{2,3},{4,5},{6,7},{8,9},{10,11},{12,13},{14,15},{16,17},{18,... | collective-permute-start | bytes 2359304 | tf_op jit(solution)/shard_map/ppermute | solution.py:215
  12.0 0.0 copy-done.3
  12.0 0.0 copy-start.1
  12.0 0.9 %copy-done.1 = f32[2,128,128]{2,1,0:T(8,128)S(1)} copy-done((f32[2,128,128]{2,1,0:T(8,128)S(1)}, f32[2,128,128]{2,1,0:T(8,128)}, u32[]{:S(2)}) %copy-start.1) | copy-done | bytes 131096
  12.9 3.3 %collective-permute-start = (f32[2,2,128,128]{3,2,1,0:T(8,128)S(1)}, f32[2,2,128,128]{3,2,1,0:T(8,128)S(1)}, u32[]{:S(2)}, u32[]{:S(2)}) collective-permute-start(f32[2,2,128,128]{3,2,1,0:T(8,128)S(1)} %pad_maximum_fusion.3), channel_id=1, source_target_pairs={{0,1},{1,0},{2,3},{3,2},{4,5},{5,4},{6,7},{7,6},{8,9},{9,8},{10,11... | collective-permute-start | bytes 786440 | tf_op jit(solution)/shard_map/ppermute | solution.py:206
  16.2 1.3 %collective-permute-done = f32[2,2,128,128]{3,2,1,0:T(8,128)S(1)} collective-permute-done((f32[2,2,128,128]{3,2,1,0:T(8,128)S(1)}, f32[2,2,128,128]{3,2,1,0:T(8,128)S(1)}, u32[]{:S(2)}, u32[]{:S(2)}) %collective-permute-start) | collective-permute-done | bytes 262176 | tf_op jit(solution)/shard_map/ppermute | solution.py:206
  17.5 4.4 %collective-permute-start.1 = (f32[2,128,128]{2,1,0:T(8,128)S(1)}, f32[2,128,128]{2,1,0:T(8,128)S(1)}, u32[]{:S(2)}, u32[]{:S(2)}) collective-permute-start(f32[2,128,128]{2,1,0:T(8,128)S(1)} %fusion.41), channel_id=1, source_target_pairs={{0,2},{1,225},{2,0},{3,227},{4,6},{5,229},{6,4},{7,231},{8,10},{9,... | collective-permute-start | bytes 393224 | tf_op jit(solution)/shard_map/ppermute | solution.py:280
  21.9 0.0 copy-start
  21.9 6.1 %tile0.1 = (f32[1024,128]{1,0:T(8,128)}, f32[1024,128]{1,0:T(8,128)}, f32[1024,128]{1,0:T(8,128)}, f32[1024,128]{1,0:T(8,128)}) custom-call(f32[2,1024,21]{2,1,0:T(8,128)} %get-tuple-element.73.w_in, bf16[1024,256]{1,0:T(8,128)(2,1)} %q.8, bf16[1024,256]{1,0:T(8,128)(2,1)} %k.5, bf16[1024,256]{1,0:T(8,128)(2,1)} %v.5, bf16[1024,256]{1,0:T(8,128)(2,1)} %g.8), custom_call_target="tpu_custom_call" | custom-call | flops 402653184 | bytes 3145728 | tf_op jit(solution)/shard_map/tile0/pallas_call | solution.py:227
  28.0 0.0 collective-permute-done.1
  28.0 0.0 collective-permute-done.2
  28.0 0.0 copy-done
  28.1 2.2 %collective-permute-start.3 = (f32[2,128,128]{2,1,0:T(8,128)S(1)}, f32[2,128,128]{2,1,0:T(8,128)S(1)}, u32[]{:S(2)}, u32[]{:S(2)}) collective-permute-start(f32[2,128,128]{2,1,0:T(8,128)S(1)} %get-tuple-element.61), channel_id=1, source_target_pairs={{0,6},{1,65},{2,4},{3,67},{4,2},{5,69},{6,0},{7,71},{8,14},{9,73},... | collective-permute-start | bytes 393224 | tf_op jit(solution)/shard_map/ppermute | solution.py:280
  30.3 6.0 %tile1.1 = (f32[1024,128]{1,0:T(8,128)}, f32[1024,128]{1,0:T(8,128)}, f32[1024,128]{1,0:T(8,128)}, f32[1024,128]{1,0:T(8,128)}) custom-call(f32[2,1024,21]{2,1,0:T(8,128)} %get-tuple-element.73.w_in, bf16[1024,256]{1,0:T(8,128)(2,1)} %q.8, bf16[1024,256]{1,0:T(8,128)(2,1)} %k.5, bf16[1024,256]{1,0:T(8,128)(2,1)} %v.5, bf16[1024,256]{1,0:T(8,128)(2,1)} %g.8), custom_call_target="tpu_custom_call" | custom-call | flops 402653184 | bytes 3145728 | tf_op jit(solution)/shard_map/tile1/pallas_call | solution.py:227
  36.3 0.0 collective-permute-done.3
  36.3 0.1 collective-permute-start.4
  36.4 3.8 %collective-permute-done.4 = f32[2,128,128]{2,1,0:T(8,128)S(1)} collective-permute-done((f32[2,128,128]{2,1,0:T(8,128)S(1)}, f32[2,128,128]{2,1,0:T(8,128)S(1)}, u32[]{:S(2)}, u32[]{:S(2)}) %collective-permute-start.4) | collective-permute-done | bytes 131104 | tf_op jit(solution)/shard_map/ppermute | solution.py:280
  40.2 3.0 %collective-permute-start.5 = (f32[2,128,128]{2,1,0:T(8,128)S(1)}, f32[2,128,128]{2,1,0:T(8,128)S(1)}, u32[]{:S(2)}, u32[]{:S(2)}) collective-permute-start(f32[2,128,128]{2,1,0:T(8,128)S(1)} %get-tuple-element.98), channel_id=1, source_target_pairs={{0,24},{1,25},{2,26},{3,27},{4,28},{5,29},{6,30},{7,31},{8,16},{9,... | collective-permute-start | bytes 393224 | tf_op jit(solution)/shard_map/ppermute | solution.py:280
  43.2 2.4 %collective-permute-done.5 = f32[2,128,128]{2,1,0:T(8,128)S(1)} collective-permute-done((f32[2,128,128]{2,1,0:T(8,128)S(1)}, f32[2,128,128]{2,1,0:T(8,128)S(1)}, u32[]{:S(2)}, u32[]{:S(2)}) %collective-permute-start.5) | collective-permute-done | bytes 131104 | tf_op jit(solution)/shard_map/ppermute | solution.py:280
  45.6 1.3 %collective-permute-start.7 = (f32[4,2,128,128]{3,2,1,0:T(8,128)S(1)}, f32[4,2,128,128]{3,2,1,0:T(8,128)S(1)}, u32[]{:S(2)}, u32[]{:S(2)}) collective-permute-start(f32[4,2,128,128]{3,2,1,0:T(8,128)S(1)} %pad_maximum_fusion), channel_id=1, source_target_pairs={{0,1},{2,3},{4,5},{6,7},{8,9},{10,11},{12,13},{14,15},{16,17},{18,... | collective-permute-start | bytes 1572872 | tf_op jit(solution)/shard_map/ppermute | solution.py:288
  47.0 0.1 collective-permute-start.6
  47.1 3.8 %collective-permute-done.6 = f32[2,128,128]{2,1,0:T(8,128)S(1)} collective-permute-done((f32[2,128,128]{2,1,0:T(8,128)S(1)}, f32[2,128,128]{2,1,0:T(8,128)S(1)}, u32[]{:S(2)}, u32[]{:S(2)}) %collective-permute-start.6) | collective-permute-done | bytes 131104 | tf_op jit(solution)/shard_map/ppermute | solution.py:280
  50.9 0.0 collective-permute-done.7
  51.0 0.0 copy-start.2
  51.1 2.6 %collective-permute-start.8 = (f32[2,128,128]{2,1,0:T(8,128)S(1)}, f32[2,128,128]{2,1,0:T(8,128)S(1)}, u32[]{:S(2)}, u32[]{:S(2)}) collective-permute-start(f32[2,128,128]{2,1,0:T(8,128)S(1)} %get-tuple-element.72), channel_id=1, source_target_pairs={{0,64},{1,7},{2,66},{3,5},{4,68},{5,3},{6,70},{7,1},{8,72},{9,15},... | collective-permute-start | bytes 393224 | tf_op jit(solution)/shard_map/ppermute | solution.py:280
  53.6 0.0 copy-done.2
  53.6 4.7 %far.1 = (f32[1024,256]{1,0:T(8,128)}, f32[1024,256]{1,0:T(8,128)}) custom-call(f32[2,1024,21]{2,1,0:T(8,128)} %get-tuple-element.73.w_in, bf16[1024,256]{1,0:T(8,128)(2,1)} %q.8, bf16[1024,256]{1,0:T(8,128)(2,1)} %g.8, f32[5,2,128,128]{3,2,1,0:T(8,128)} %copy-done.2), custom_call_target="tpu_custom_call" | custom-call | flops 671088640 | bytes 3145728 | tf_op jit(solution)/shard_map/far/pallas_call | solution.py:246
  58.4 0.0 collective-permute-done.8
  58.4 0.3 collective-permute-start.9
  58.7 3.6 %collective-permute-done.9 = f32[2,128,128]{2,1,0:T(8,128)S(1)} collective-permute-done((f32[2,128,128]{2,1,0:T(8,128)S(1)}, f32[2,128,128]{2,1,0:T(8,128)S(1)}, u32[]{:S(2)}, u32[]{:S(2)}) %collective-permute-start.9) | collective-permute-done | bytes 131104 | tf_op jit(solution)/shard_map/ppermute | solution.py:280
  62.4 5.7 %collective-permute-start.10 = (f32[3,2,128,128]{3,2,1,0:T(8,128)S(1)}, f32[3,2,128,128]{3,2,1,0:T(8,128)S(1)}, u32[]{:S(2)}, u32[]{:S(2)}) collective-permute-start(f32[3,2,128,128]{3,2,1,0:T(8,128)S(1)} %pad_maximum_fusion.1), channel_id=1, source_target_pairs={{0,1},{1,0},{2,3},{3,2},{4,5},{5,4},{6,7},{7,6},{8,9},{9,8},{10,11... | collective-permute-start | bytes 1179656 | tf_op jit(solution)/shard_map/ppermute | solution.py:294
  68.1 1.3 %collective-permute-done.10 = f32[3,2,128,128]{3,2,1,0:T(8,128)S(1)} collective-permute-done((f32[3,2,128,128]{3,2,1,0:T(8,128)S(1)}, f32[3,2,128,128]{3,2,1,0:T(8,128)S(1)}, u32[]{:S(2)}, u32[]{:S(2)}) %collective-permute-start.10) | collective-permute-done | bytes 393248 | tf_op jit(solution)/shard_map/ppermute | solution.py:294
  69.4 0.7 add_select_fusion
  70.2 0.8 pad_maximum_fusion.2.buckets
  70.9 6.7 %last.1 = (f32[1024,256]{1,0:T(8,128)}, f32[1024,256]{1,0:T(8,128)}, f32[1024,256]{1,0:T(8,128)}, f32[1024,256]{1,0:T(8,128)}) custom-call(f32[2,1024,21]{2,1,0:T(8,128)} %get-tuple-element.73.w_in, bf16[1024,256]{1,0:T(8,128)(2,1)} %q.8, bf16[1024,256]{1,0:T(8,128)(2,1)} %k.5, bf16[1024,256]{1,0:T(8,128)(2,1)} %v.5, bf16[1024,256]{1,0:T(8,128)(2,1)} %g.8, ...), custom_call_target="tpu_custom_call" | custom-call | flops 536870912 | bytes 10485760 | tf_op jit(solution)/shard_map/last/pallas_call | solution.py:305
  (17 shorter events, 0.5 us)
Async XLA Ops:
  6.2 5.8 %copy-start.3 = (f32[2,2,128,128]{3,2,1,0:T(8,128)S(1)}, f32[2,2,128,128]{3,2,1,0:T(8,128)}, u32[]{:S(2)}) copy-start(f32[2,2,128,128]{3,2,1,0:T(8,128)} %get-tuple-element.49) | copy-start | bytes 786436
  10.7 17.4 %collective-permute-start.2 = (f32[6,2,128,128]{3,2,1,0:T(8,128)}, f32[6,2,128,128]{3,2,1,0:T(8,128)S(1)}, u32[]{:S(2)}, u32[]{:S(2)}) collective-permute-start(f32[6,2,128,128]{3,2,1,0:T(8,128)} %second.1), channel_id=1, source_target_pairs={{0,1},{2,3},{4,5},{6,7},{8,9},{10,11},{12,13},{14,15},{16,17},{18,... | collective-permute-start | bytes 2359304 | tf_op jit(solution)/shard_map/ppermute | solution.py:215
  12.0 0.9 %copy-start.1 = (f32[2,128,128]{2,1,0:T(8,128)S(1)}, f32[2,128,128]{2,1,0:T(8,128)}, u32[]{:S(2)}) copy-start(f32[2,128,128]{2,1,0:T(8,128)} %get-tuple-element.48) | copy-start | bytes 393220
  12.9 4.6 %collective-permute-start = (f32[2,2,128,128]{3,2,1,0:T(8,128)S(1)}, f32[2,2,128,128]{3,2,1,0:T(8,128)S(1)}, u32[]{:S(2)}, u32[]{:S(2)}) collective-permute-start(f32[2,2,128,128]{3,2,1,0:T(8,128)S(1)} %pad_maximum_fusion.3), channel_id=1, source_target_pairs={{0,1},{1,0},{2,3},{3,2},{4,5},{5,4},{6,7},{7,6},{8,9},{9,8},{10,11... | collective-permute-start | bytes 786440 | tf_op jit(solution)/shard_map/ppermute | solution.py:206
  17.5 10.5 %collective-permute-start.1 = (f32[2,128,128]{2,1,0:T(8,128)S(1)}, f32[2,128,128]{2,1,0:T(8,128)S(1)}, u32[]{:S(2)}, u32[]{:S(2)}) collective-permute-start(f32[2,128,128]{2,1,0:T(8,128)S(1)} %fusion.41), channel_id=1, source_target_pairs={{0,2},{1,225},{2,0},{3,227},{4,6},{5,229},{6,4},{7,231},{8,10},{9,... | collective-permute-start | bytes 393224 | tf_op jit(solution)/shard_map/ppermute | solution.py:280
  21.9 6.1 %copy-start = (f32[6,2,128,128]{3,2,1,0:T(8,128)S(1)}, f32[6,2,128,128]{3,2,1,0:T(8,128)}, u32[]{:S(2)}) copy-start(f32[6,2,128,128]{3,2,1,0:T(8,128)} %second.1) | copy-start | bytes 2359300
  28.1 8.2 %collective-permute-start.3 = (f32[2,128,128]{2,1,0:T(8,128)S(1)}, f32[2,128,128]{2,1,0:T(8,128)S(1)}, u32[]{:S(2)}, u32[]{:S(2)}) collective-permute-start(f32[2,128,128]{2,1,0:T(8,128)S(1)} %get-tuple-element.61), channel_id=1, source_target_pairs={{0,6},{1,65},{2,4},{3,67},{4,2},{5,69},{6,0},{7,71},{8,14},{9,73},... | collective-permute-start | bytes 393224 | tf_op jit(solution)/shard_map/ppermute | solution.py:280
  36.3 3.9 %collective-permute-start.4 = (f32[2,128,128]{2,1,0:T(8,128)S(1)}, f32[2,128,128]{2,1,0:T(8,128)S(1)}, u32[]{:S(2)}, u32[]{:S(2)}) collective-permute-start(f32[2,128,128]{2,1,0:T(8,128)S(1)} %get-tuple-element.100), channel_id=1, source_target_pairs={{0,8},{1,33},{2,10},{3,35},{4,12},{5,37},{6,14},{7,39},{8,0},{9,41... | collective-permute-start | bytes 393224 | tf_op jit(solution)/shard_map/ppermute | solution.py:280
  40.2 5.4 %collective-permute-start.5 = (f32[2,128,128]{2,1,0:T(8,128)S(1)}, f32[2,128,128]{2,1,0:T(8,128)S(1)}, u32[]{:S(2)}, u32[]{:S(2)}) collective-permute-start(f32[2,128,128]{2,1,0:T(8,128)S(1)} %get-tuple-element.98), channel_id=1, source_target_pairs={{0,24},{1,25},{2,26},{3,27},{4,28},{5,29},{6,30},{7,31},{8,16},{9,... | collective-permute-start | bytes 393224 | tf_op jit(solution)/shard_map/ppermute | solution.py:280
  45.6 5.3 %collective-permute-start.7 = (f32[4,2,128,128]{3,2,1,0:T(8,128)S(1)}, f32[4,2,128,128]{3,2,1,0:T(8,128)S(1)}, u32[]{:S(2)}, u32[]{:S(2)}) collective-permute-start(f32[4,2,128,128]{3,2,1,0:T(8,128)S(1)} %pad_maximum_fusion), channel_id=1, source_target_pairs={{0,1},{2,3},{4,5},{6,7},{8,9},{10,11},{12,13},{14,15},{16,17},{18,... | collective-permute-start | bytes 1572872 | tf_op jit(solution)/shard_map/ppermute | solution.py:288
  47.0 3.9 %collective-permute-start.6 = (f32[2,128,128]{2,1,0:T(8,128)S(1)}, f32[2,128,128]{2,1,0:T(8,128)S(1)}, u32[]{:S(2)}, u32[]{:S(2)}) collective-permute-start(f32[2,128,128]{2,1,0:T(8,128)S(1)} %get-tuple-element.96), channel_id=1, source_target_pairs={{0,32},{1,9},{2,34},{3,11},{4,36},{5,13},{6,38},{7,15},{8,40},{9,1... | collective-permute-start | bytes 393224 | tf_op jit(solution)/shard_map/ppermute | solution.py:280
  51.0 2.6 %copy-start.2 = (f32[5,2,128,128]{3,2,1,0:T(8,128)}, f32[5,2,128,128]{3,2,1,0:T(8,128)S(1)}, u32[]{:S(2)}) copy-start(f32[5,2,128,128]{3,2,1,0:T(8,128)S(1)} %fusion.12.buckets) | copy-start | bytes 1966084
  51.1 7.3 %collective-permute-start.8 = (f32[2,128,128]{2,1,0:T(8,128)S(1)}, f32[2,128,128]{2,1,0:T(8,128)S(1)}, u32[]{:S(2)}, u32[]{:S(2)}) collective-permute-start(f32[2,128,128]{2,1,0:T(8,128)S(1)} %get-tuple-element.72), channel_id=1, source_target_pairs={{0,64},{1,7},{2,66},{3,5},{4,68},{5,3},{6,70},{7,1},{8,72},{9,15},... | collective-permute-start | bytes 393224 | tf_op jit(solution)/shard_map/ppermute | solution.py:280
  58.4 3.9 %collective-permute-start.9 = (f32[2,128,128]{2,1,0:T(8,128)S(1)}, f32[2,128,128]{2,1,0:T(8,128)S(1)}, u32[]{:S(2)}, u32[]{:S(2)}) collective-permute-start(f32[2,128,128]{2,1,0:T(8,128)S(1)} %get-tuple-element.92), channel_id=1, source_target_pairs={{0,224},{1,3},{2,226},{3,1},{4,228},{5,7},{6,230},{7,5},{8,232},{9... | collective-permute-start | bytes 393224 | tf_op jit(solution)/shard_map/ppermute | solution.py:280
  62.4 7.1 %collective-permute-start.10 = (f32[3,2,128,128]{3,2,1,0:T(8,128)S(1)}, f32[3,2,128,128]{3,2,1,0:T(8,128)S(1)}, u32[]{:S(2)}, u32[]{:S(2)}) collective-permute-start(f32[3,2,128,128]{3,2,1,0:T(8,128)S(1)} %pad_maximum_fusion.1), channel_id=1, source_target_pairs={{0,1},{1,0},{2,3},{3,2},{4,5},{5,4},{6,7},{7,6},{8,9},{9,8},{10,11... | collective-permute-start | bytes 1179656 | tf_op jit(solution)/shard_map/ppermute | solution.py:294
